TPU v7x, 512 devices: a whole 4x8x8 slice. The times are simulated.
512 devices in a mesh: row: 16 (over x, y_lo), col: 16 (over z, core), dp: 2 (over y_hi).
Axes of the slice: x: 4, y: 8 (y_hi: 2, y_lo: 4; y = y_hi * 4 + y_lo), z: 8, core: 2. Of those that a mesh axis runs over, the one named last changes fastest.
Arguments:
- grad_output: bfloat16 [2, 2048, 8192], P('dp', 'col', 'row'), may hold values from -0.09375 to 0.09375
- block_input: bfloat16 [2, 2048, 8192], P('dp', 'col', 'row'), may hold values from -6 to 6
- query_branch: bfloat16 [2, 2048, 8192], P('dp', 'row', 'col'), may hold values from -6 to 6
- key_branch: bfloat16 [2, 2048, 8192], P('dp', 'row', 'col'), may hold values from -6 to 6
- value_branch: bfloat16 [2, 2048, 8192], P('dp', 'row', 'col'), may hold values from -6 to 6
- out_weight: bfloat16 [8192, 8192], P('row', 'col'), may hold values from -0.0625 to 0.0625
- filters: float32 [512, 128], P('col'), may hold values from -0.5 to 0.5
Outputs:
- out_weight_grad: float32 [8192, 8192], P('row', 'col')
- value_weight_grad: float32 [8192, 8192], P('col', 'row')
- filter_grad: float32 [512, 128], P('col')
All inputs are finite; a program needn't handle non-finite values.
Results may differ from a plain program's by a relative error of at most 0.0029.
Values may be sent and summed in bfloat16 or wider, within the bound.
A program may use at most 128 MiB of HBM per device.

v0:
```python
import jax
import jax.numpy as jnp
from jax import lax
from jax.sharding import PartitionSpec as P

highest = lax.Precision.HIGHEST


def toeplitz(taps, tok_rows, causal):
    filter_len = taps.shape[1]
    out_pos = lax.broadcasted_iota(jnp.int32, (tok_rows, tok_rows + filter_len), 0)
    in_pos = lax.broadcasted_iota(jnp.int32, (tok_rows, tok_rows + filter_len), 1)
    lagged = out_pos + filter_len - in_pos if causal else in_pos - out_pos
    inside = (lagged >= 0) & (lagged < filter_len)
    picked = jnp.take(taps, jnp.clip(lagged, 0, filter_len - 1), axis=1)
    return jnp.where(inside[None], picked, 0.0)


def grouped_apply(table, signal, groups):
    blocks, extent, channels = signal.shape
    split = signal.reshape(blocks, extent, groups, channels // groups)
    result = jnp.einsum("gts,bsgc->btgc", table, split, precision=highest)
    return result.reshape(blocks, table.shape[1], channels)


def taps_partial(delta_mix, mixed_ext, groups, filter_len):
    blocks, tok_rows, channels = delta_mix.shape
    left_side = delta_mix.reshape(blocks, tok_rows, groups, channels // groups)
    right_side = mixed_ext.reshape(blocks, tok_rows + filter_len, groups, channels // groups)
    products = jnp.einsum("btgc,bsgc->gts", left_side, right_side, precision=highest)
    extent = tok_rows + filter_len
    flipped = products[:, :, ::-1]
    padded = jnp.pad(flipped, ((0, 0), (0, 0), (0, tok_rows)))
    flat_rows = padded.reshape(groups, -1)[:, : tok_rows * (extent + tok_rows - 1)]
    skewed = flat_rows.reshape(groups, tok_rows, extent + tok_rows - 1)
    column_sums = jnp.sum(skewed, axis=1)
    return column_sums[:, tok_rows - 1 : tok_rows - 1 + filter_len]


def local(grad_output, block_input, query_branch, key_branch, value_branch, out_weight, filters):
    filter_len = filters.shape[1]
    groups = filters.shape[0]
    tok_rows = query_branch.shape[1]
    channels = query_branch.shape[2]
    grads_all, inputs_all = (
        lax.all_gather(grad_output[0], "col", axis=0, tiled=True),
        lax.all_gather(block_input[0], "col", axis=0, tiled=True),
    )
    row_devices = lax.axis_size("row")
    sub_width = channels // row_devices
    delta_turned = lax.psum_scatter(
        lax.dot_general(
            out_weight, grads_all, (((0,), (1,)), ((), ())), preferred_element_type=jnp.float32
        ),
        "row",
        scatter_dimension=0,
        tiled=True,
    )
    queries, keys_here, values_here = (
        lax.all_to_all(query_branch[0], "row", split_axis=1, concat_axis=0, tiled=True),
        lax.all_to_all(key_branch[0], "row", split_axis=1, concat_axis=0, tiled=True),
        lax.all_to_all(value_branch[0], "row", split_axis=1, concat_axis=0, tiled=True),
    )
    delta_out = delta_turned.T
    local_groups = sub_width // (channels // groups)
    first_group = lax.axis_index("row") * local_groups
    my_taps = lax.dynamic_slice_in_dim(filters, first_group, local_groups, 0)
    mixed = keys_here.astype(jnp.float32) * values_here.astype(jnp.float32)
    mixed_blocks = mixed.reshape(row_devices, tok_rows, sub_width)
    earlier = jnp.concatenate(
        [
            jnp.zeros((1, filter_len, sub_width), jnp.float32),
            mixed_blocks[:-1, tok_rows - filter_len :],
        ],
        axis=0,
    )
    mixed_ext = jnp.concatenate([earlier, mixed_blocks], axis=1)
    conv_out = grouped_apply(toeplitz(my_taps, tok_rows, True), mixed_ext, local_groups).reshape(
        -1, sub_width
    )
    gated = (queries.astype(jnp.float32) * conv_out).astype(jnp.bfloat16)
    delta_mix = delta_out * queries.astype(jnp.float32)
    delta_blocks = delta_mix.reshape(row_devices, tok_rows, sub_width)
    later_part = jnp.concatenate(
        [delta_blocks[1:, :filter_len], jnp.zeros((1, filter_len, sub_width), jnp.float32)], axis=0
    )
    delta_ext = jnp.concatenate([delta_blocks, later_part], axis=1)
    delta_conv = grouped_apply(toeplitz(my_taps, tok_rows, False), delta_ext, local_groups).reshape(
        -1, sub_width
    )
    delta_value = (delta_conv * keys_here.astype(jnp.float32)).astype(jnp.bfloat16)
    my_terms = taps_partial(delta_blocks, mixed_ext, local_groups, filter_len)
    taps_local = lax.dynamic_update_slice_in_dim(
        jnp.zeros(filters.shape, jnp.float32), my_terms, first_group, 0
    )
    gated_all, value_all = (
        lax.all_gather(gated, "row", axis=1, tiled=True),
        lax.all_gather(delta_value, "row", axis=1, tiled=True),
    )
    out_grad = lax.dot_general(
        grads_all, gated_all, (((0,), (0,)), ((), ())), preferred_element_type=jnp.float32
    )
    value_grad = lax.dot_general(
        value_all, inputs_all, (((0,), (0,)), ((), ())), preferred_element_type=jnp.float32
    )
    out_grad, value_grad = lax.psum((out_grad, value_grad), "dp")
    taps_total = lax.psum(taps_local, ("row", "dp"))
    return (out_grad, value_grad, taps_total)


def solution(mesh):
    in_specs = (
        P("dp", "col", "row"),
        P("dp", "col", "row"),
        P("dp", "row", "col"),
        P("dp", "row", "col"),
        P("dp", "row", "col"),
        P("row", "col"),
        P("col", None),
    )
    out_specs = (P("row", "col"), P("col", "row"), P("col", None))
    return jax.shard_map(local, mesh=mesh, in_specs=in_specs, out_specs=out_specs, check_vma=False)
```

profile of v0, /device:TPU:64, one launch (start us, length us, event | category | flops | bytes accessed | tf_op | source)
XLA Modules:
  0.0 689.4 jit_solution(379694975442089937)
XLA Ops:
  7.2 0.7 all-gather.11.cloned.1.call-update
  8.0 48.5 %all-gather.11.cloned.1.call-done = bf16[1,2048,512]{2,1,0:T(8,128)(2,1)} async-done(((bf16[1,128,512]{2,1,0:T(8,128)(2,1)}), bf16[1,2048,512]{2,1,0:T(8,128)(2,1)}) %all-gather.11.cloned.1.call-update) | async-done | bytes 2097168 | tf_op jit(solution)/shard_map/all_gather | solution.py:46
  56.5 4.8 fusion.2
  61.4 0.9 copy-done.2
  62.2 0.8 copy.40
  63.0 7.1 %all-to-all-start.2 = ((bf16[128,16,32]{0,2,1:T(8,128)(2,1)}), bf16[128,16,32]{0,2,1:T(8,128)(2,1)S(1)}, u32[]{:S(2)}, u32[]{:S(2)}) async-start(bf16[128,16,32]{0,2,1:T(8,128)(2,1)} %bitcast.4), calls=%async_computation.2 | async-start | bytes 262144 | tf_op jit(solution)/shard_map/all_to_all | solution.py:62
  70.1 0.1 fusion.30
  70.3 0.1 copy.66
  70.4 0.7 constant_dynamic-slice_fusion
  71.1 0.8 copy.38
  71.8 0.1 copy.62
  71.9 109.0 %gather_fusion = f32[32768,2]{1,0:T(8,128)} fusion(f32[2,128]{0,1:T(8,128)S(1)} %copy.62, s32[32768]{0:T(1024)S(1)} %broadcast_clamp_fusion.1), kind=kCustom, calls=%fused_computation.clone | custom fusion | bytes 655360 | tf_op jit(solution)/shard_map/jit(_take)/gather | solution.py:15
  180.9 10.0 %copy.46 = f32[128,256,2]{1,0,2:T(8,128)S(1)} copy(f32[128,256,2]{2,1,0:T(8,128)} %bitcast.113) | data formatting | bytes 524288 | tf_op jit(solution)/shard_map/jit(_take)/gather | solution.py:15
  190.9 0.8 copy.36
  191.7 0.2 fusion.35
  191.9 7.5 %all-to-all-start.1 = ((bf16[128,16,32]{0,2,1:T(8,128)(2,1)}), bf16[128,16,32]{0,2,1:T(8,128)(2,1)S(1)}, u32[]{:S(2)}, u32[]{:S(2)}) async-start(bf16[128,16,32]{0,2,1:T(8,128)(2,1)} %bitcast.2), calls=%async_computation.1 | async-start | bytes 262144 | tf_op jit(solution)/shard_map/all_to_all | solution.py:61
  199.4 8.4 %all-to-all-done.1 = bf16[128,16,32]{0,2,1:T(8,128)(2,1)S(1)} async-done(((bf16[128,16,32]{0,2,1:T(8,128)(2,1)}), bf16[128,16,32]{0,2,1:T(8,128)(2,1)S(1)}, u32[]{:S(2)}, u32[]{:S(2)}) %all-to-all-start.1) | async-done | bytes 131104 | tf_op jit(solution)/shard_map/all_to_all | solution.py:61
  207.8 3.5 all-to-all-start
  211.3 0.0 all-gather.7.cloned.1.call-start
  211.4 0.1 slice.19
  211.5 0.1 copy_dynamic-update-slice_fusion
  211.7 0.6 convolution_bitcast_fusion.2
  212.3 0.1 copy.47
  212.4 7.3 %all-to-all-done = bf16[128,16,32]{0,2,1:T(8,128)(2,1)S(1)} async-done(((bf16[128,16,32]{0,2,1:T(8,128)(2,1)}), bf16[128,16,32]{0,2,1:T(8,128)(2,1)S(1)}, u32[]{:S(2)}, u32[]{:S(2)}) %all-to-all-start) | async-done | bytes 131104 | tf_op jit(solution)/shard_map/all_to_all | solution.py:60
  219.6 1.7 bitcast_multiply_fusion.2
  221.4 0.5 all-gather.13.cloned.1.call-update
  222.0 0.1 copy.69
  222.2 109.0 %gather_fusion.1 = f32[32768,2]{1,0:T(8,128)} fusion(f32[2,128]{0,1:T(8,128)S(1)} %copy.62, s32[32768]{0:T(1024)S(1)} %broadcast_clamp_fusion), kind=kCustom, calls=%fused_computation.1.clone | custom fusion | bytes 655360 | tf_op jit(solution)/shard_map/jit(_take)/gather | solution.py:15
  331.2 10.1 %copy.51 = f32[128,256,2]{1,0,2:T(8,128)S(1)} copy(f32[128,256,2]{2,1,0:T(8,128)} %bitcast.112) | data formatting | bytes 524288 | tf_op jit(solution)/shard_map/jit(_take)/gather | solution.py:15
  341.2 0.1 fusion.34
  341.3 0.1 slice.21
  341.4 0.1 copy.50
  341.6 0.1 copy.49
  341.7 0.6 convolution_bitcast_fusion.1
  342.3 0.1 copy.52
  342.4 0.7 fusion.13
  343.2 4.5 fusion.6
  347.7 1.5 all-gather.13.cloned.1.call-done
  349.2 91.4 %all-gather.9.cloned.1.call-done = bf16[2048,512]{0,1:T(8,128)(2,1)} async-done(((bf16[2048,32]{0,1:T(8,128)(2,1)}), bf16[2048,512]{0,1:T(8,128)(2,1)}) %all-gather.9.cloned.1.call-update) | async-done | bytes 2097168 | tf_op jit(solution)/shard_map/all_gather | solution.py:98
  440.6 4.4 fusion
  445.1 0.8 convolution_bitcast_fusion
  445.9 0.4 rev.3
  446.3 0.3 copy.71
  446.7 0.6 reshape.76
  447.3 0.1 slice_dynamic-update-slice_fusion
  447.4 231.5 %psum.23 = f32[32,128]{1,0:T(8,128)} all-reduce(f32[32,128]{1,0:T(8,128)S(1)} %slice_dynamic-update-slice_fusion), channel_id=1, replica_groups=mesh['row'=16,'col'=16,'dp'=2] {'row','dp'}, use_global_device_ids=true, to_apply=%region_4.6 | all-reduce | flops 4096 | bytes 32768 | tf_op jit(solution)/shard_map/psum | solution.py:107
  678.9 2.6 copy.54
  681.5 1.0 copy.88
  (39 shorter events, 0.7 us)
Async XLA Ops:
  7.2 49.3 %copy-start = (bf16[512,512]{1,0:T(8,128)(2,1)S(1)}, bf16[512,512]{1,0:T(8,128)(2,1)}, u32[]{:S(2)}) copy-start(bf16[512,512]{1,0:T(8,128)(2,1)} %param.14) | copy-start | bytes 1572868
  7.2 49.3 %all-gather.11.cloned.1.call-start = ((), (), s32[]{:S(2)}) async-start(), calls=%async_computation.7 | async-start | bytes 2228224 | tf_op jit(solution)/shard_map/all_gather | solution.py:46
  7.9 211.7 %reduce-scatter.2.cloned.1.call-start = ((), (), s32[]{:S(2)}) async-start(), calls=%async_computation.5 | async-start | bytes 4456448 | tf_op jit(solution)/shard_map/reduce_scatter | solution.py:51
  61.3 0.9 copy-start.2
  61.3 9.7 %copy-start.3 = (bf16[1,128,512]{2,1,0:T(8,128)(2,1)S(1)}, bf16[1,128,512]{2,1,0:T(8,128)(2,1)}, u32[]{:S(2)}) copy-start(bf16[1,128,512]{2,1,0:T(8,128)(2,1)} %param.12) | copy-start | bytes 393220
  63.0 128.9 %all-to-all-start.2 = ((bf16[128,16,32]{0,2,1:T(8,128)(2,1)}), bf16[128,16,32]{0,2,1:T(8,128)(2,1)S(1)}, u32[]{:S(2)}, u32[]{:S(2)}) async-start(bf16[128,16,32]{0,2,1:T(8,128)(2,1)} %bitcast.4), calls=%async_computation.2 | async-start | bytes 262144 | tf_op jit(solution)/shard_map/all_to_all | solution.py:62
  180.9 10.0 %copy-start.4 = (bf16[1,128,512]{2,1,0:T(8,128)(2,1)S(1)}, bf16[1,128,512]{2,1,0:T(8,128)(2,1)}, u32[]{:S(2)}) copy-start(bf16[1,128,512]{2,1,0:T(8,128)(2,1)} %param.11) | copy-start | bytes 393220
  191.9 15.9 %all-to-all-start.1 = ((bf16[128,16,32]{0,2,1:T(8,128)(2,1)}), bf16[128,16,32]{0,2,1:T(8,128)(2,1)S(1)}, u32[]{:S(2)}, u32[]{:S(2)}) async-start(bf16[128,16,32]{0,2,1:T(8,128)(2,1)} %bitcast.2), calls=%async_computation.1 | async-start | bytes 262144 | tf_op jit(solution)/shard_map/all_to_all | solution.py:61
  207.8 11.9 %all-to-all-start = ((bf16[128,16,32]{0,2,1:T(8,128)(2,1)}), bf16[128,16,32]{0,2,1:T(8,128)(2,1)S(1)}, u32[]{:S(2)}, u32[]{:S(2)}) async-start(bf16[128,16,32]{0,2,1:T(8,128)(2,1)} %bitcast), calls=%async_computation | async-start | bytes 262144 | tf_op jit(solution)/shard_map/all_to_all | solution.py:60
  211.3 131.9 %all-gather.7.cloned.1.call-start = ((), (), s32[]{:S(2)}) async-start(), calls=%async_computation.4 | async-start | bytes 2228224 | tf_op jit(solution)/shard_map/all_gather | solution.py:97
  221.4 127.9 %all-gather.13.cloned.1.call-start = ((), (), s32[]{:S(2)}) async-start(), calls=%async_computation.8 | async-start | bytes 2228224 | tf_op jit(solution)/shard_map/all_gather | solution.py:47
  222.0 218.7 %all-gather.9.cloned.1.call-start = ((), (), s32[]{:S(2)}) async-start(), calls=%async_computation.6 | async-start | bytes 2228224 | tf_op jit(solution)/shard_map/all_gather | solution.py:98
  343.2 335.8 %all-reduce.6.cloned.1.call-start = ((), (), s32[]{:S(2)}) async-start(), calls=%async_computation.9 | async-start | bytes 4194304 | tf_op jit(solution)/shard_map/psum | solution.py:106
  678.9 2.6 copy-start.1
Sparse Core Ops, SparseCore 0:
  10.1 46.3 all-gather.10
  61.5 105.1 reduce-scatter.1
  221.5 84.2 all-gather.6
  307.8 41.4 all-gather.12
  351.7 88.8 all-gather.8
  445.2 122.4 all-reduce.5
where the time goes:
time: 690 us; the launch traced here: 689 us
  local copies, waits for them, and re-layouts  248 us (36%)
  blocking collectives  232 us (34%)
  waiting for transfers between devices  158 us (23%)
  starting transfers between devices  18.4 us (3%)
  matrix products  15.8 us (2%)
  between operations  14.4 us (2%)
    gather x4, local copies, waits for them, and re-layouts, toeplitz(): picked = jnp.take(taps, jnp.clip(lagged, 0, filter_len - 1), axis=1)  238 us
    psum x1, blocking collectives, local(): taps_total = lax.psum(taps_local, ('row', 'dp'))  232 us
    all_gather x1, waiting for transfers between devices, local(): lax.all_gather(delta_value, 'row', axis=1, tiled=True)  91.4 us
    all_gather x1, waiting for transfers between devices, local(): lax.all_gather(grad_output[0], 'col', axis=0, tiled=True)  48.5 us
  transfers between devices with their start and end apart: 9, of which 5 were waited for; matrix products, arithmetic and copies ran while one was open for 36% of the time, Pallas kernels for 0%

commit v1 on v0

--- a/solution.py
+++ b/solution.py
@@ -95,7 +95,9 @@
     )
     gated_all, value_all = (
         lax.all_gather(gated, "row", axis=1, tiled=True),
-        lax.all_gather(delta_value, "row", axis=1, tiled=True),
+        jnp.concatenate(
+            lax.all_to_all(jnp.stack([delta_value] * lax.axis_size("row")), "row", 0, 0), axis=1
+        ),
     )
     out_grad = lax.dot_general(
         grads_all, gated_all, (((0,), (0,)), ((), ())), preferred_element_type=jnp.float32

time: 690 us -> 641 us (0.929)
  the two profiles are of different devices: /device:TPU:64 before, /device:TPU:40 now
where the time goes in v1:
time: 641 us; the launch traced here: 640 us
  local copies, waits for them, and re-layouts  248 us (39%)
  blocking collectives  234 us (37%)
  waiting for transfers between devices  103 us (16%)
  starting transfers between devices  22.7 us (4%)
  matrix products  15.2 us (2%)
  between operations  14.1 us (2%)
    gather x4, local copies, waits for them, and re-layouts, toeplitz(): picked = jnp.take(taps, jnp.clip(lagged, 0, filter_len - 1), axis=1)  237 us
    psum x1, blocking collectives, local(): taps_total = lax.psum(taps_local, ('row', 'dp'))  234 us
    all_gather x1, waiting for transfers between devices, local(): lax.all_gather(grad_output[0], 'col', axis=0, tiled=True)  49.6 us
    all_to_all x1, waiting for transfers between devices, local(): lax.all_to_all(jnp.stack([delta_value] * lax.axis_size('row')), 'row', 0, 0)  38.9 us
  transfers between devices with their start and end apart: 9, of which 4 were waited for; matrix products, arithmetic and copies ran while one was open for 39% of the time, Pallas kernels for 0%

profile of v1, /device:TPU:40, one launch (start us, length us, event | category | flops | bytes accessed | tf_op | source)
XLA Modules:
  0.0 640.3 jit_solution(6153766318672468249)
XLA Ops:
  7.2 0.7 all-gather.8.cloned.1.call-update
  8.0 49.6 %all-gather.8.cloned.1.call-done = bf16[1,2048,512]{2,1,0:T(8,128)(2,1)} async-done(((bf16[1,128,512]{2,1,0:T(8,128)(2,1)}), bf16[1,2048,512]{2,1,0:T(8,128)(2,1)}) %all-gather.8.cloned.1.call-update) | async-done | bytes 2097168 | tf_op jit(solution)/shard_map/all_gather | solution.py:46
  57.6 4.8 fusion.2
  62.4 0.9 copy-done.2
  63.3 0.8 copy.40
  64.1 5.8 all-to-all-start.2
  69.8 0.1 fusion.30
  69.9 0.1 copy.66
  70.0 0.7 constant_dynamic-slice_fusion
  70.8 0.8 copy.38
  71.5 0.1 copy.62
  71.6 108.5 %gather_fusion = f32[32768,2]{1,0:T(8,128)} fusion(f32[2,128]{0,1:T(8,128)S(1)} %copy.62, s32[32768]{0:T(1024)S(1)} %broadcast_clamp_fusion.1), kind=kCustom, calls=%fused_computation.clone | custom fusion | bytes 655360 | tf_op jit(solution)/shard_map/jit(_take)/gather | solution.py:15
  180.1 10.0 %copy.46 = f32[128,256,2]{1,0,2:T(8,128)S(1)} copy(f32[128,256,2]{2,1,0:T(8,128)} %bitcast.116) | data formatting | bytes 524288 | tf_op jit(solution)/shard_map/jit(_take)/gather | solution.py:15
  190.1 0.8 copy.36
  190.9 0.2 fusion.35
  191.0 7.5 %all-to-all-start.1 = ((bf16[128,16,32]{0,2,1:T(8,128)(2,1)}), bf16[128,16,32]{0,2,1:T(8,128)(2,1)S(1)}, u32[]{:S(2)}, u32[]{:S(2)}) async-start(bf16[128,16,32]{0,2,1:T(8,128)(2,1)} %bitcast.2), calls=%async_computation.1 | async-start | bytes 262144 | tf_op jit(solution)/shard_map/all_to_all | solution.py:61
  198.6 7.3 %all-to-all-done.1 = bf16[128,16,32]{0,2,1:T(8,128)(2,1)S(1)} async-done(((bf16[128,16,32]{0,2,1:T(8,128)(2,1)}), bf16[128,16,32]{0,2,1:T(8,128)(2,1)S(1)}, u32[]{:S(2)}, u32[]{:S(2)}) %all-to-all-start.1) | async-done | bytes 131104 | tf_op jit(solution)/shard_map/all_to_all | solution.py:61
  205.8 4.5 all-to-all-start
  210.5 0.1 slice.19
  210.6 0.1 copy_dynamic-update-slice_fusion
  210.7 0.6 convolution_bitcast_fusion.2
  211.4 0.1 copy.47
  211.5 6.3 all-to-all-done
  217.7 1.7 bitcast_multiply_fusion.2
  219.5 0.5 all-gather.10.cloned.1.call-update
  220.1 0.1 fusion.34
  220.2 0.1 copy.69
  220.3 108.5 %gather_fusion.1 = f32[32768,2]{1,0:T(8,128)} fusion(f32[2,128]{0,1:T(8,128)S(1)} %copy.62, s32[32768]{0:T(1024)S(1)} %broadcast_clamp_fusion), kind=kCustom, calls=%fused_computation.1.clone | custom fusion | bytes 655360 | tf_op jit(solution)/shard_map/jit(_take)/gather | solution.py:15
  328.8 10.1 %copy.51 = f32[128,256,2]{1,0,2:T(8,128)S(1)} copy(f32[128,256,2]{2,1,0:T(8,128)} %bitcast.115) | data formatting | bytes 524288 | tf_op jit(solution)/shard_map/jit(_take)/gather | solution.py:15
  338.9 0.1 slice.21
  338.9 0.1 copy.50
  339.1 0.1 copy.49
  339.2 0.6 convolution_bitcast_fusion.1
  339.8 0.1 copy.52
  339.9 0.1 fusion.13
  340.0 1.6 stack.2
  341.6 4.7 all-to-all-start.3
  346.3 4.5 fusion.6
  350.8 38.9 %all-to-all-done.3 = bf16[16,2048,32]{1,2,0:T(8,128)(2,1)S(1)} async-done(((bf16[16,2048,32]{1,2,0:T(8,128)(2,1)}), bf16[16,2048,32]{1,2,0:T(8,128)(2,1)S(1)}, u32[]{:S(2)}, u32[]{:S(2)}) %all-to-all-start.3) | async-done | bytes 2097184 | tf_op jit(solution)/shard_map/all_to_all | solution.py:99
  389.7 3.8 fusion
  393.6 0.8 convolution_bitcast_fusion
  394.4 0.4 rev.3
  394.8 0.3 copy.71
  395.1 0.5 reshape.89
  395.7 0.1 slice_dynamic-update-slice_fusion
  395.8 234.3 %psum.23 = f32[32,128]{1,0:T(8,128)} all-reduce(f32[32,128]{1,0:T(8,128)S(1)} %slice_dynamic-update-slice_fusion), channel_id=1, replica_groups=mesh['row'=16,'col'=16,'dp'=2] {'row','dp'}, use_global_device_ids=true, to_apply=%region_4.6 | all-reduce | flops 4096 | bytes 32768 | tf_op jit(solution)/shard_map/psum | solution.py:109
  630.1 2.6 copy.54
  632.8 1.0 copy.88
  (39 shorter events, 0.7 us)
Async XLA Ops:
  7.2 50.4 %copy-start = (bf16[512,512]{1,0:T(8,128)(2,1)S(1)}, bf16[512,512]{1,0:T(8,128)(2,1)}, u32[]{:S(2)}) copy-start(bf16[512,512]{1,0:T(8,128)(2,1)} %param.14) | copy-start | bytes 1572868
  7.2 50.4 %all-gather.8.cloned.1.call-start = ((), (), s32[]{:S(2)}) async-start(), calls=%async_computation.7 | async-start | bytes 2228224 | tf_op jit(solution)/shard_map/all_gather | solution.py:46
  7.9 209.8 %reduce-scatter.2.cloned.1.call-start = ((), (), s32[]{:S(2)}) async-start(), calls=%async_computation.6 | async-start | bytes 4456448 | tf_op jit(solution)/shard_map/reduce_scatter | solution.py:51
  62.4 0.9 copy-start.2
  62.4 8.4 %copy-start.3 = (bf16[1,128,512]{2,1,0:T(8,128)(2,1)S(1)}, bf16[1,128,512]{2,1,0:T(8,128)(2,1)}, u32[]{:S(2)}) copy-start(bf16[1,128,512]{2,1,0:T(8,128)(2,1)} %param.12) | copy-start | bytes 393220
  64.1 127.0 %all-to-all-start.2 = ((bf16[128,16,32]{0,2,1:T(8,128)(2,1)}), bf16[128,16,32]{0,2,1:T(8,128)(2,1)S(1)}, u32[]{:S(2)}, u32[]{:S(2)}) async-start(bf16[128,16,32]{0,2,1:T(8,128)(2,1)} %bitcast.4), calls=%async_computation.2 | async-start | bytes 262144 | tf_op jit(solution)/shard_map/all_to_all | solution.py:62
  180.1 10.0 %copy-start.4 = (bf16[1,128,512]{2,1,0:T(8,128)(2,1)S(1)}, bf16[1,128,512]{2,1,0:T(8,128)(2,1)}, u32[]{:S(2)}) copy-start(bf16[1,128,512]{2,1,0:T(8,128)(2,1)} %param.11) | copy-start | bytes 393220
  191.0 14.8 %all-to-all-start.1 = ((bf16[128,16,32]{0,2,1:T(8,128)(2,1)}), bf16[128,16,32]{0,2,1:T(8,128)(2,1)S(1)}, u32[]{:S(2)}, u32[]{:S(2)}) async-start(bf16[128,16,32]{0,2,1:T(8,128)(2,1)} %bitcast.2), calls=%async_computation.1 | async-start | bytes 262144 | tf_op jit(solution)/shard_map/all_to_all | solution.py:61
  205.8 11.9 %all-to-all-start = ((bf16[128,16,32]{0,2,1:T(8,128)(2,1)}), bf16[128,16,32]{0,2,1:T(8,128)(2,1)S(1)}, u32[]{:S(2)}, u32[]{:S(2)}) async-start(bf16[128,16,32]{0,2,1:T(8,128)(2,1)} %bitcast), calls=%async_computation | async-start | bytes 262144 | tf_op jit(solution)/shard_map/all_to_all | solution.py:60
  210.4 136.0 %all-gather.6.cloned.1.call-start = ((), (), s32[]{:S(2)}) async-start(), calls=%async_computation.5 | async-start | bytes 2228224 | tf_op jit(solution)/shard_map/all_gather | solution.py:97
  219.5 131.3 %all-gather.10.cloned.1.call-start = ((), (), s32[]{:S(2)}) async-start(), calls=%async_computation.8 | async-start | bytes 2228224 | tf_op jit(solution)/shard_map/all_gather | solution.py:47
  341.6 48.1 %all-to-all-start.3 = ((bf16[16,2048,32]{1,2,0:T(8,128)(2,1)}), bf16[16,2048,32]{1,2,0:T(8,128)(2,1)S(1)}, u32[]{:S(2)}, u32[]{:S(2)}) async-start(bf16[16,2048,32]{1,2,0:T(8,128)(2,1)} %stack.2), calls=%async_computation.4 | async-start | bytes 4194304 | tf_op jit(solution)/shard_map/all_to_all | solution.py:99
  346.3 283.9 %all-reduce.6.cloned.1.call-start = ((), (), s32[]{:S(2)}) async-start(), calls=%async_computation.9 | async-start | bytes 4194304 | tf_op jit(solution)/shard_map/psum | solution.py:108
  630.1 2.6 copy-start.1
Sparse Core Ops, SparseCore 0:
  10.1 47.3 all-gather.7
  62.5 100.3 reduce-scatter.1
  219.6 84.8 all-gather.5
  306.4 43.7 all-gather.9
  393.7 126.0 all-reduce.5
